TPU v7x, 32 devices: a whole 2x2x4 slice. The times are simulated.
32 devices in a mesh: mem: 8 (over z, y), lat: 4 (over x, core).
Axes of the slice: x: 2, y: 2, z: 4, core: 2. Of those that a mesh axis runs over, the one named last changes fastest.
Arguments:
- prior_state: bfloat16 [512, 64, 8, 128], P('mem', None, 'lat'), may hold values from -6 to 6
- norm_scale: float32 [64], replicated, may hold values from 0.1 to 1.9
- entry_kernel: bfloat16 [9, 256, 64], replicated, may hold values from -0.25 to 0.25
- closing_filter: bfloat16 [9, 64, 256], replicated, may hold values from -0.125 to 0.125
- observed_cell: int32 [8, 4, 16], P('mem', 'lat'), may hold values from 0 to 31
- observed_weight: float32 [8, 4, 16, 64], P('mem', 'lat'), may hold values from -0.75 to 0.75
- observed_value: float32 [8, 4, 16], P('mem', 'lat'), may hold values from -6 to 6
- observed_precision: float32 [8, 4, 16], P('mem', 'lat'), may hold values from 0.25 to 2
Outputs:
- analysed: float32 [128, 8, 64, 512], P('mem', 'lat')
Inputs may be any that keep to these rules, and one draw needn't show every extreme that they name: observed_cell is (column within the 16 columns of its group) * 2 + (row within its band).
All inputs are finite; a program needn't handle non-finite values.
Results may differ from a plain program's by a relative error of at most 0.0036.
Values may be sent and summed in bfloat16 or wider, within the bound.
A program may use at most 128 MiB of HBM per device.

v0:
```python
import functools
import math

import jax
import jax.numpy as jnp
from jax import lax
from jax.experimental import pallas as pl
from jax.experimental.pallas import tpu as pltpu
from jax.sharding import PartitionSpec as P

NS_ITERS = 3
LANES = 128
MESH = pl.DeviceIdType.MESH
VMEM_LIMIT = 56 * 1024 * 1024
F32 = jnp.float32
BF16 = jnp.bfloat16
highest = lax.Precision.HIGHEST


def halo_kernel(own_ref, below_ref, above_ref, send_sem, recv_sem):
    bands = lax.axis_size("lat")
    band = lax.axis_index("lat")
    barrier = pltpu.get_barrier_semaphore()

    @pl.when(band > 0)
    def _():
        pl.semaphore_signal(barrier, inc=1, device_id={"lat": band - 1}, device_id_type=MESH)

    @pl.when(band < bands - 1)
    def _():
        pl.semaphore_signal(barrier, inc=1, device_id={"lat": band + 1}, device_id_type=MESH)

    peers = jnp.where(band > 0, 1, 0) + jnp.where(band < bands - 1, 1, 0)
    pl.semaphore_wait(barrier, peers)

    down = pltpu.make_async_remote_copy(
        own_ref, above_ref, send_sem.at[0], recv_sem.at[0],
        device_id={"lat": band - 1}, device_id_type=MESH,
    )
    up = pltpu.make_async_remote_copy(
        own_ref, below_ref, send_sem.at[1], recv_sem.at[1],
        device_id={"lat": band + 1}, device_id_type=MESH,
    )

    @pl.when(band > 0)
    def _():
        down.start()

    @pl.when(band < bands - 1)
    def _():
        up.start()

    @pl.when(band > 0)
    def _():
        down.wait_send()
        up.wait_recv()

    @pl.when(band < bands - 1)
    def _():
        up.wait_send()
        down.wait_recv()


def halo_exchange(own):
    shape = jax.ShapeDtypeStruct(own.shape, own.dtype)
    anywhere = pl.BlockSpec(memory_space=pl.ANY)
    return pl.pallas_call(
        halo_kernel,
        out_shape=(shape, shape),
        in_specs=[anywhere],
        out_specs=(anywhere, anywhere),
        scratch_shapes=[pltpu.SemaphoreType.DMA((2,)), pltpu.SemaphoreType.DMA((2,))],
        compiler_params=pltpu.CompilerParams(collective_id=0, has_side_effects=True),
        name="halo",
    )(own)


def greet_all(axis):
    count = lax.axis_size(axis)
    me = lax.axis_index(axis)
    barrier = pltpu.get_barrier_semaphore()
    for step in range(1, count):
        pl.semaphore_signal(
            barrier, inc=1, device_id={axis: lax.rem(me + step, count)}, device_id_type=MESH
        )
    pl.semaphore_wait(barrier, count - 1)


def exchange_kernel(parts_ref, got_ref, send_sem, recv_sem, own_sem):
    count = lax.axis_size("mem")
    me = lax.axis_index("mem")
    greet_all("mem")
    copies = []
    for step in range(1, count):
        other = lax.rem(me + step, count)
        copy = pltpu.make_async_remote_copy(
            parts_ref.at[other], got_ref.at[me], send_sem.at[step], recv_sem.at[step],
            device_id={"mem": other}, device_id_type=MESH,
        )
        copy.start()
        copies.append(copy)
    keep = pltpu.make_async_copy(parts_ref.at[me], got_ref.at[me], own_sem)
    keep.start()
    keep.wait()
    for copy in copies:
        copy.wait()


def exchange(parts):
    count = parts.shape[0]
    anywhere = pl.BlockSpec(memory_space=pl.ANY)
    return pl.pallas_call(
        exchange_kernel,
        out_shape=jax.ShapeDtypeStruct(parts.shape, parts.dtype),
        in_specs=[anywhere],
        out_specs=anywhere,
        scratch_shapes=[
            pltpu.SemaphoreType.DMA((count,)),
            pltpu.SemaphoreType.DMA((count,)),
            pltpu.SemaphoreType.DMA,
        ],
        compiler_params=pltpu.CompilerParams(collective_id=1, has_side_effects=True),
        name="exchange",
    )(parts)


def gather_kernel(mine_ref, all_ref, send_sem, recv_sem, own_sem):
    count = lax.axis_size("mem")
    me = lax.axis_index("mem")
    greet_all("mem")
    copies = []
    for step in range(1, count):
        other = lax.rem(me + step, count)
        copy = pltpu.make_async_remote_copy(
            mine_ref, all_ref.at[me], send_sem.at[step], recv_sem.at[step],
            device_id={"mem": other}, device_id_type=MESH,
        )
        copy.start()
        copies.append(copy)
    keep = pltpu.make_async_copy(mine_ref, all_ref.at[me], own_sem)
    keep.start()
    keep.wait()
    for copy in copies:
        copy.wait()


def gather(mine, count):
    return pl.pallas_call(
        gather_kernel,
        out_shape=jax.ShapeDtypeStruct((count,) + mine.shape, mine.dtype),
        in_specs=[pl.BlockSpec(memory_space=pltpu.VMEM)],
        out_specs=pl.BlockSpec(memory_space=pltpu.VMEM),
        scratch_shapes=[
            pltpu.SemaphoreType.DMA((count,)),
            pltpu.SemaphoreType.DMA((count,)),
            pltpu.SemaphoreType.DMA,
        ],
        compiler_params=pltpu.CompilerParams(collective_id=2, has_side_effects=True),
        name="gather",
    )(mine)


def forecast_kernel(
    groups, own_ref, below_ref, above_ref, gain_ref, entry_ref, closing_ref,
    parts_ref, stack, field,
):
    members, rows, width = own_ref.shape
    band = lax.axis_index("lat")
    bands = lax.axis_size("lat")
    has_below = band > 0
    has_above = band < bands - 1
    gain = gain_ref[...]
    half_below = jnp.where(has_below, 0.5, 0.0).astype(F32)
    half_above = jnp.where(has_above, 0.5, 0.0).astype(F32)

    def normed(ref, member):
        values = ref[member].astype(F32).reshape(rows // 8, 8, width)
        square = jnp.sum(values * values, axis=0)
        square = square + pltpu.roll(square, 2, 0)
        square = square + pltpu.roll(square, 4, 0)
        inverse = lax.rsqrt(square * (2.0 / rows) + 1e-06)
        return (values * inverse[None]).reshape(rows, width) * gain

    def gelu(value, half):
        inner = math.sqrt(2.0 / math.pi) * (value + 0.044715 * (value * value * value))
        return ((half * value) * (1.0 + jnp.tanh(inner))).astype(BF16)

    pair = 2
    half_rows = entry_ref.shape[0] // 2
    depth = entry_ref.shape[1] // 2
    for first in range(0, members, pair):
        for which in range(pair):
            lanes = slice(which * width, (which + 1) * width)
            for block, (ref, valid) in enumerate(
                ((below_ref, has_below), (own_ref, None), (above_ref, has_above))
            ):
                value = normed(ref, first + which)
                if valid is not None:
                    value = jnp.where(valid, value, 0.0)
                for tap in range(3):
                    moved = value if tap == 1 else pltpu.roll(value, (1 - tap) % width, 1)
                    start = block * depth + tap * rows
                    stack[start : start + rows, lanes] = moved.astype(BF16)
        entry = entry_ref[...]
        low = jnp.dot(entry, stack[: 2 * depth, :], preferred_element_type=F32)
        high = jnp.dot(entry, stack[depth:, :], preferred_element_type=F32)
        hidden = jnp.concatenate(
            [
                gelu(low[:half_rows], half_below),
                gelu(low[half_rows:], 0.5),
                gelu(high[:half_rows], 0.5),
                gelu(high[half_rows:], half_above),
            ],
            axis=0,
        )
        products = jnp.dot(closing_ref[...], hidden, preferred_element_type=F32)
        for which in range(pair):
            lanes = slice(which * width, (which + 1) * width)
            total = own_ref[first + which].astype(F32)
            for tap in range(3):
                part = products[tap * rows : (tap + 1) * rows, lanes]
                total = total + (part if tap == 1 else pltpu.roll(part, (1 - tap) % width, 1))
            field[(first + which) * rows : (first + which + 1) * rows, :] = total

    columns = width // groups
    lane_group = lax.broadcasted_iota(jnp.int32, (members, width), 1) // columns
    pieces = rows // (2 * groups)
    for piece in range(pieces):
        for line in range(2):
            tiles = [
                field[pl.ds(piece * groups * 2 + inner * 2 + line, members, stride=rows), :]
                for inner in range(groups)
            ]
            step = 1
            while step < groups:
                keep_low = (lane_group // step) % 2 == 0
                turned = list(tiles)
                for index in range(groups):
                    if (index // step) % 2 == 0:
                        a, b = tiles[index], tiles[index + step]
                        turned[index] = jnp.where(keep_low, a, pltpu.roll(b, step * columns, 1))
                        turned[index + step] = jnp.where(
                            keep_low, pltpu.roll(a, width - step * columns, 1), b
                        )
                tiles = turned
                step *= 2
            for group in range(groups):
                parts_ref[group, piece * 2 + line] = tiles[group].astype(BF16)


def forecast(own, below, above, gain, entry, closing, groups):
    members, rows, width = own.shape
    chunk = min(16, members)
    pieces = rows // groups
    block = pl.BlockSpec((chunk, rows, width), lambda i: (i, 0, 0))
    whole = lambda a: pl.BlockSpec(a.shape, lambda i: (0,) * a.ndim)
    return pl.pallas_call(
        functools.partial(forecast_kernel, groups),
        out_shape=jax.ShapeDtypeStruct((groups, pieces, members, width), BF16),
        grid=(members // chunk,),
        in_specs=[block, block, block, whole(gain), whole(entry), whole(closing)],
        out_specs=pl.BlockSpec((groups, pieces, chunk, width), lambda i: (0, 0, i, 0)),
        scratch_shapes=[
            pltpu.VMEM((9 * rows, 2 * width), BF16),
            pltpu.VMEM((chunk * rows, width), F32),
        ],
        compiler_params=pltpu.CompilerParams(vmem_limit_bytes=VMEM_LIMIT),
        name="forecast",
    )(own, below, above, gain, entry, closing)


def observe_kernel(got_ref, operator_ref, value_ref, precision_ref, out_ref):
    sources, pieces, part, width = got_ref.shape
    observations = operator_ref.shape[1]
    total = None
    for piece in range(pieces):
        operator = operator_ref[piece]
        high = operator.astype(BF16)
        rest = operator - high.astype(F32)
        middle = rest.astype(BF16)
        low = (rest - middle.astype(F32)).astype(BF16)
        stacked = jnp.concatenate([high, middle, low], axis=0)
        states = got_ref[:, piece].reshape(sources * part, width)
        term = lax.dot_general(
            stacked, states, (((1,), (1,)), ((), ())), preferred_element_type=F32
        )
        total = term if total is None else total + term
    seen = total[:observations] + (total[observations : 2 * observations] + total[2 * observations :])
    mean = jnp.mean(seen, axis=1, keepdims=True)
    root = jnp.sqrt(precision_ref[...])
    out_ref[:, : sources * part] = (seen - mean) * root[:, :1]
    out_ref[:, sources * part :] = (value_ref[...] - mean) * root


def observe(got, operator, value, precision):
    sources, _, part, width = got.shape
    observations = operator.shape[1]
    return pl.pallas_call(
        observe_kernel,
        out_shape=jax.ShapeDtypeStruct((observations, sources * part + LANES), F32),
        compiler_params=pltpu.CompilerParams(vmem_limit_bytes=VMEM_LIMIT),
        name="observe",
    )(got, operator, value, precision)


def weights_of(gathered, members):
    u = gathered[:, :members] * (1.0 / math.sqrt(members - 1))
    innovation = gathered[:, members:]
    count = u.shape[0]
    dot = functools.partial(jnp.dot, precision=highest, preferred_element_type=F32)
    g = lax.dot_general(u, u, (((1,), (1,)), ((), ())), precision=highest, preferred_element_type=F32)
    eye = (
        lax.broadcasted_iota(jnp.int32, (count, count), 0)
        == lax.broadcasted_iota(jnp.int32, (count, count), 1)
    ).astype(F32)
    total = lambda a: jnp.sum(jnp.sum(a, axis=1, keepdims=True), axis=0, keepdims=True)
    square = total(g * (g + 2.0 * eye)) + float(members)
    magnitude = jnp.sqrt(square)
    y_c, y_m = 1.0 / magnitude, eye / magnitude
    z_c, z_m = jnp.ones_like(magnitude), None
    for sweep in range(NS_ITERS):
        if z_m is None:
            p_m = y_m
        else:
            gy = dot(g, y_m)
            p_m = z_c * y_m + y_c * z_m + dot(z_m, gy)
        t_c, t_m = 0.5 * (3.0 - z_c * y_c), -0.5 * p_m
        gt = dot(g, t_m)
        if sweep + 1 < NS_ITERS:
            y_c, y_m = y_c * t_c, y_c * t_m + t_c * y_m + dot(y_m, gt)
        if z_m is None:
            z_c, z_m = t_c * z_c, z_c * t_m
        else:
            z_c, z_m = t_c * z_c, t_c * z_m + z_c * t_m + dot(z_m, gt)
    scale = lax.rsqrt(magnitude)
    a_c, a_m = z_c * scale, z_m * scale
    once = a_c * innovation + dot(a_m, dot(g, innovation))
    twice = a_c * once + dot(a_m, dot(g, once))
    v = dot(a_m, u) + twice[:, :1] * (1.0 / math.sqrt(members - 1))
    full = lax.dot_general(u, v, (((0,), (0,)), ((), ())), precision=highest, preferred_element_type=F32)
    diagonal = lax.broadcasted_iota(jnp.int32, (members, members), 0) == lax.broadcasted_iota(
        jnp.int32, (members, members), 1
    )
    full = full + jnp.where(diagonal, a_c, 0.0)
    column = jnp.sum(full, axis=0, keepdims=True)
    return full + (1.0 - column) * (1.0 / members)


def analyse_kernel(got_ref, gathered_ref, out_ref, coarse, fine, turned):
    sources, _, part, width = got_ref.shape
    members = sources * part
    columns, lines, inner, _ = out_ref.shape

    @pl.when(pl.program_id(0) == 0)
    def _():
        full = weights_of(gathered_ref[...], members)
        high = full.astype(BF16)
        coarse[...] = high
        fine[...] = (full - high.astype(F32)).astype(BF16)

    turn = (((0,), (0,)), ((), ()))
    for line in range(lines):
        states = got_ref[:, line].reshape(members, width)
        result = lax.dot_general(states, coarse[...], turn, preferred_element_type=F32)
        result += lax.dot_general(states, fine[...], turn, preferred_element_type=F32)
        for index in range(inner):
            rows = result[index * columns : (index + 1) * columns]
            for tile in range(members // LANES):
                turned[tile, pl.ds(line * inner + index, columns, stride=lines * inner), :] = rows[
                    :, tile * LANES : (tile + 1) * LANES
                ]
    for tile in range(members // LANES):
        out_ref[:, :, :, tile * LANES : (tile + 1) * LANES] = turned[tile].reshape(
            columns, lines, inner, LANES
        )


def analyse(got, gathered, columns, variables):
    sources, _, part, width = got.shape
    members = sources * part
    inner = width // columns
    return pl.pallas_call(
        analyse_kernel,
        out_shape=jax.ShapeDtypeStruct((columns, 2, variables, members), F32),
        grid=(variables // inner,),
        in_specs=[
            pl.BlockSpec((sources, 2, part, width), lambda i: (0, i, 0, 0)),
            pl.BlockSpec(gathered.shape, lambda i: (0, 0)),
        ],
        out_specs=pl.BlockSpec((columns, 2, inner, members), lambda i: (0, 0, i, 0)),
        scratch_shapes=[
            pltpu.VMEM((members, members), BF16),
            pltpu.VMEM((members, members), BF16),
            pltpu.VMEM((members // LANES, columns * 2 * inner, LANES), F32),
        ],
        compiler_params=pltpu.CompilerParams(vmem_limit_bytes=VMEM_LIMIT),
        name="analyse",
    )(got, gathered)


def on_device(
    prior_state,
    norm_scale,
    entry_kernel,
    closing_filter,
    observed_cell,
    observed_weight,
    observed_value,
    observed_precision,
):
    groups = lax.axis_size("mem")
    members, variables, lines, width = prior_state.shape
    hidden = entry_kernel.shape[1]
    columns = width // groups
    own = prior_state.reshape(members, variables * lines, width)
    gain = jnp.broadcast_to(jnp.repeat(norm_scale, lines)[:, None], (variables * lines, width))

    taps = entry_kernel.reshape(3, 3, hidden, variables)
    by_line = jnp.stack([jnp.pad(taps, ((j, 1 - j), (0, 0), (0, 0), (0, 0))) for j in range(2)])
    entry = by_line.reshape(2, 2, 2, 3, hidden, variables)
    entry = jnp.transpose(entry, (0, 4, 1, 3, 5, 2)).reshape(2 * hidden, 12 * variables)
    taps = closing_filter.reshape(3, 3, variables, hidden)
    by_line = jnp.stack([jnp.pad(taps, ((y, 1 - y), (0, 0), (0, 0), (0, 0))) for y in range(2)])
    closing = jnp.transpose(by_line, (2, 3, 0, 1, 4)).reshape(6 * variables, 4 * hidden)

    located = observed_cell[0, 0]
    observations = located.shape[0]
    cells = (located[:, None] == lax.iota(jnp.int32, columns * lines)[None, :]).astype(F32)
    cells = jnp.transpose(cells.reshape(observations, columns, lines), (2, 0, 1))
    weight = observed_weight[0, 0].reshape(observations, variables // groups, groups)
    operator = (
        jnp.transpose(weight, (1, 0, 2))[:, None, :, :, None] * cells[None, :, :, None, :]
    ).reshape(variables // groups * lines, observations, groups * columns)
    value = jnp.broadcast_to(observed_value[0, 0][:, None], (observations, LANES))
    precision = jnp.broadcast_to(observed_precision[0, 0][:, None], (observations, LANES))

    below, above = halo_exchange(own)
    parts = forecast(own, below, above, gain, entry, closing, groups)
    got = exchange(parts)
    mine = observe(got, operator, value, precision)
    gathered = gather(mine, groups)
    gathered = gathered.reshape(groups * observations, mine.shape[1])
    return analyse(got, gathered, columns, variables)


def solution(mesh):
    return jax.shard_map(
        on_device,
        mesh=mesh,
        in_specs=(
            P("mem", None, "lat", None),
            P(),
            P(),
            P(),
            P("mem", "lat", None),
            P("mem", "lat", None, None),
            P("mem", "lat", None),
            P("mem", "lat", None),
        ),
        out_specs=P("mem", "lat", None, None),
        check_vma=False,
    )
```

profile of v0, /device:TPU:1, one launch (start us, length us, event | category | flops | bytes accessed | tf_op | source)
XLA Modules:
  0.0 127.3 jit_solution(884779633222912682)
XLA Ops:
  0.0 1.1 fusion
  1.1 0.1 maximum_bitcast_fusion
  1.2 0.8 copy.12
  2.0 0.2 copy.18
  2.2 0.0 copy-start
  2.2 1.2 copy.15.entry_ref
  3.4 26.7 %halo.1 = (bf16[64,128,128]{2,1,0:T(8,128)(2,1)}, bf16[64,128,128]{2,1,0:T(8,128)(2,1)}) custom-call(bf16[64,128,128]{2,1,0:T(8,128)(2,1)} %bitcast.29), custom_call_target="tpu_custom_call" | custom-call | tf_op jit(solution)/shard_map/halo/pallas_call | solution.py:67
  30.0 0.0 copy-done
  30.1 0.3 copy.13
  30.3 0.0 copy-start.2
  30.3 0.4 pad_bitcast_fusion.1
  30.7 0.5 pad_maximum_fusion
  31.2 1.1 copy.19
  32.3 0.0 copy-done.2
  32.3 0.1 broadcast_in_dim.27
  32.4 0.1 broadcast_in_dim.28
  32.5 0.7 broadcast_in_dim.29.gain_ref
  33.2 34.7 %forecast.1.parts_ref = bf16[8,16,64,128]{3,2,1,0:T(8,128)(2,1)} custom-call(bf16[64,128,128]{2,1,0:T(8,128)(2,1)} %bitcast.30, bf16[64,128,128]{2,1,0:T(8,128)(2,1)} %get-tuple-element.7.below_ref, bf16[64,128,128]{2,1,0:T(8,128)(2,1)} %get-tuple-element.8.above_ref, f32[128,128]{1,0:T(8,128)} %broadcast_in_dim.29.gain_ref, ...), custom_call_target="tpu_custom_call" | custom-call | tf_op jit(solution)/shard_map/forecast/pallas_call | solution.py:257
  68.0 23.0 %exchange.1.got_ref = bf16[8,16,64,128]{3,2,1,0:T(8,128)(2,1)} custom-call(bf16[8,16,64,128]{3,2,1,0:T(8,128)(2,1)} %forecast.1.parts_ref), custom_call_target="tpu_custom_call" | custom-call | tf_op jit(solution)/shard_map/exchange/pallas_call | solution.py:112
  91.0 0.0 copy-start.4
  91.0 0.0 copy-start.5
  91.0 0.1 copy.16
  91.1 0.1 copy.17
  91.2 0.1 compare_convert_fusion
  91.2 0.2 broadcast_multiply_fusion
  91.5 1.0 mul.20.operator_ref
  92.4 0.0 copy-done.4
  92.4 0.7 broadcast_in_dim.31.value_ref
  93.1 0.7 broadcast_in_dim.33.precision_ref
  93.8 3.1 %observe.1.mine_ref = f32[16,640]{1,0:T(8,128)} custom-call(bf16[8,16,64,128]{3,2,1,0:T(8,128)(2,1)} %exchange.1.got_ref, f32[16,16,128]{2,1,0:T(8,128)} %mul.20.operator_ref, f32[16,128]{1,0:T(8,128)} %broadcast_in_dim.31.value_ref, f32[16,128]{1,0:T(8,128)} %broadcast_in_dim.33.precision_ref), custom_call_target="tpu_custom_call" | custom-call | tf_op jit(solution)/shard_map/observe/pallas_call | solution.py:298
  96.8 17.0 %gather.1 = f32[8,16,640]{2,1,0:T(8,128)} custom-call(f32[16,640]{1,0:T(8,128)} %observe.1.mine_ref), custom_call_target="tpu_custom_call" | custom-call | tf_op jit(solution)/shard_map/gather/pallas_call | solution.py:148
  113.8 13.5 %analyse.1 = f32[16,2,64,512]{3,2,1,0:T(8,128)} custom-call(bf16[8,16,64,128]{3,2,1,0:T(8,128)(2,1)} %exchange.1.got_ref, f32[128,640]{1,0:T(8,128)} %bitcast.37), custom_call_target="tpu_custom_call" | custom-call | tf_op jit(solution)/shard_map/analyse/pallas_call | solution.py:382
  (6 shorter events, 0.0 us)
Async XLA Ops:
  2.2 27.8 %copy-start = (bf16[9,64,256]{2,1,0:T(8,128)(2,1)S(1)}, bf16[9,64,256]{2,1,0:T(8,128)(2,1)}, u32[]{:S(2)}) copy-start(bf16[9,64,256]{2,1,0:T(8,128)(2,1)} %param.11) | copy-start | bytes 884740
  30.3 2.0 %copy-start.2 = (f32[64]{0:T(128)S(1)}, f32[64]{0:T(128)}, u32[]{:S(2)}) copy-start(f32[64]{0:T(128)} %param.9) | copy-start | bytes 772
  68.0 23.0 %copy-start.1 = (f32[1,1,16,64]{3,2,1,0:T(8,128)S(1)}, f32[1,1,16,64]{3,2,1,0:T(8,128)}, u32[]{:S(2)}) copy-start(f32[1,1,16,64]{3,2,1,0:T(8,128)} %param.13) | copy-start | bytes 12292
  68.0 23.2 %copy-start.3 = (s32[1,1,16]{2,1,0:T(1,128)S(1)}, s32[1,1,16]{2,1,0:T(1,128)}, u32[]{:S(2)}) copy-start(s32[1,1,16]{2,1,0:T(1,128)} %param.12) | copy-start | bytes 196
  91.0 1.5 %copy-start.4 = (f32[1,1,16]{2,1,0:T(1,128)S(1)}, f32[1,1,16]{2,1,0:T(1,128)}, u32[]{:S(2)}) copy-start(f32[1,1,16]{2,1,0:T(1,128)} %param.14) | copy-start | bytes 196
  91.0 2.1 %copy-start.5 = (f32[1,1,16]{2,1,0:T(1,128)S(1)}, f32[1,1,16]{2,1,0:T(1,128)}, u32[]{:S(2)}) copy-start(f32[1,1,16]{2,1,0:T(1,128)} %param.15) | copy-start | bytes 196
where the time goes:
time: 130 us; the launch traced here: 127 us
  Pallas kernels  118 us (91%)
  local copies, waits for them, and re-layouts  8.36 us (6%)
    pallas_call x1, Pallas kernels, forecast(): pl.pallas_call(functools.partial(forecast_kernel, groups), out_shape=jax....  34.7 us
    pallas_call x1, Pallas kernels, halo_exchange(): pl.pallas_call(halo_kernel, out_shape=(shape, shape), in_specs=[anywhere]...  26.7 us
    pallas_call x1, Pallas kernels, exchange(): pl.pallas_call(exchange_kernel, out_shape=jax.ShapeDtypeStruct(parts.shap...  23 us
    pallas_call x1, Pallas kernels, gather(): pl.pallas_call(gather_kernel, out_shape=jax.ShapeDtypeStruct((count,) + m...  17 us
    pallas_call x1, Pallas kernels, analyse(): pl.pallas_call(analyse_kernel, out_shape=jax.ShapeDtypeStruct((columns, 2...  13.5 us
    pallas_call x1, Pallas kernels, observe(): pl.pallas_call(observe_kernel, out_shape=jax.ShapeDtypeStruct((observatio...  3.08 us

commit v1 on v0

--- a/solution.py
+++ b/solution.py
@@ -17,64 +17,6 @@
 highest = lax.Precision.HIGHEST
 
 
-def halo_kernel(own_ref, below_ref, above_ref, send_sem, recv_sem):
-    bands = lax.axis_size("lat")
-    band = lax.axis_index("lat")
-    barrier = pltpu.get_barrier_semaphore()
-
-    @pl.when(band > 0)
-    def _():
-        pl.semaphore_signal(barrier, inc=1, device_id={"lat": band - 1}, device_id_type=MESH)
-
-    @pl.when(band < bands - 1)
-    def _():
-        pl.semaphore_signal(barrier, inc=1, device_id={"lat": band + 1}, device_id_type=MESH)
-
-    peers = jnp.where(band > 0, 1, 0) + jnp.where(band < bands - 1, 1, 0)
-    pl.semaphore_wait(barrier, peers)
-
-    down = pltpu.make_async_remote_copy(
-        own_ref, above_ref, send_sem.at[0], recv_sem.at[0],
-        device_id={"lat": band - 1}, device_id_type=MESH,
-    )
-    up = pltpu.make_async_remote_copy(
-        own_ref, below_ref, send_sem.at[1], recv_sem.at[1],
-        device_id={"lat": band + 1}, device_id_type=MESH,
-    )
-
-    @pl.when(band > 0)
-    def _():
-        down.start()
-
-    @pl.when(band < bands - 1)
-    def _():
-        up.start()
-
-    @pl.when(band > 0)
-    def _():
-        down.wait_send()
-        up.wait_recv()
-
-    @pl.when(band < bands - 1)
-    def _():
-        up.wait_send()
-        down.wait_recv()
-
-
-def halo_exchange(own):
-    shape = jax.ShapeDtypeStruct(own.shape, own.dtype)
-    anywhere = pl.BlockSpec(memory_space=pl.ANY)
-    return pl.pallas_call(
-        halo_kernel,
-        out_shape=(shape, shape),
-        in_specs=[anywhere],
-        out_specs=(anywhere, anywhere),
-        scratch_shapes=[pltpu.SemaphoreType.DMA((2,)), pltpu.SemaphoreType.DMA((2,))],
-        compiler_params=pltpu.CompilerParams(collective_id=0, has_side_effects=True),
-        name="halo",
-    )(own)
-
-
 def greet_all(axis):
     count = lax.axis_size(axis)
     me = lax.axis_index(axis)
@@ -84,44 +26,6 @@
             barrier, inc=1, device_id={axis: lax.rem(me + step, count)}, device_id_type=MESH
         )
     pl.semaphore_wait(barrier, count - 1)
-
-
-def exchange_kernel(parts_ref, got_ref, send_sem, recv_sem, own_sem):
-    count = lax.axis_size("mem")
-    me = lax.axis_index("mem")
-    greet_all("mem")
-    copies = []
-    for step in range(1, count):
-        other = lax.rem(me + step, count)
-        copy = pltpu.make_async_remote_copy(
-            parts_ref.at[other], got_ref.at[me], send_sem.at[step], recv_sem.at[step],
-            device_id={"mem": other}, device_id_type=MESH,
-        )
-        copy.start()
-        copies.append(copy)
-    keep = pltpu.make_async_copy(parts_ref.at[me], got_ref.at[me], own_sem)
-    keep.start()
-    keep.wait()
-    for copy in copies:
-        copy.wait()
-
-
-def exchange(parts):
-    count = parts.shape[0]
-    anywhere = pl.BlockSpec(memory_space=pl.ANY)
-    return pl.pallas_call(
-        exchange_kernel,
-        out_shape=jax.ShapeDtypeStruct(parts.shape, parts.dtype),
-        in_specs=[anywhere],
-        out_specs=anywhere,
-        scratch_shapes=[
-            pltpu.SemaphoreType.DMA((count,)),
-            pltpu.SemaphoreType.DMA((count,)),
-            pltpu.SemaphoreType.DMA,
-        ],
-        compiler_params=pltpu.CompilerParams(collective_id=1, has_side_effects=True),
-        name="exchange",
-    )(parts)
 
 
 def gather_kernel(mine_ref, all_ref, send_sem, recv_sem, own_sem):
@@ -161,20 +65,91 @@
 
 
 def forecast_kernel(
-    groups, own_ref, below_ref, above_ref, gain_ref, entry_ref, closing_ref,
-    parts_ref, stack, field,
+    own_ref, gain_ref, entry_ref, closing_ref, prior_ref, got_ref,
+    below_ref, above_ref, parts_ref, stack, field,
+    halo_send, halo_recv, part_send, part_recv, keep_sem,
 ):
     members, rows, width = own_ref.shape
+    chunks = pl.num_programs(0)
+    chunk_count = parts_ref.shape[0]
+    chunk = pl.program_id(0)
+    groups = lax.axis_size("mem")
+    me = lax.axis_index("mem")
     band = lax.axis_index("lat")
     bands = lax.axis_size("lat")
     has_below = band > 0
     has_above = band < bands - 1
+
+    def to_lower(index):
+        piece = pl.ds(index * members, members)
+        return pltpu.make_async_remote_copy(
+            prior_ref.at[piece], above_ref.at[piece], halo_send.at[0, index], halo_recv.at[0, index],
+            device_id={"lat": band - 1}, device_id_type=MESH,
+        )
+
+    def to_upper(index):
+        piece = pl.ds(index * members, members)
+        return pltpu.make_async_remote_copy(
+            prior_ref.at[piece], below_ref.at[piece], halo_send.at[1, index], halo_recv.at[1, index],
+            device_id={"lat": band + 1}, device_id_type=MESH,
+        )
+
+    def to_group(index, step):
+        other = lax.rem(me + step, groups)
+        return pltpu.make_async_remote_copy(
+            parts_ref.at[index, other], got_ref.at[me, :, pl.ds(index * members, members)],
+            part_send.at[index, step], part_recv.at[index, step],
+            device_id={"mem": other}, device_id_type=MESH,
+        )
+
+    def to_self(index):
+        return pltpu.make_async_copy(
+            parts_ref.at[index, me], got_ref.at[me, :, pl.ds(index * members, members)],
+            keep_sem.at[index],
+        )
+
+    @pl.when(chunk == 0)
+    def _():
+        barrier = pltpu.get_barrier_semaphore()
+        for step in range(1, groups):
+            pl.semaphore_signal(
+                barrier, inc=1, device_id={"mem": lax.rem(me + step, groups)}, device_id_type=MESH
+            )
+
+        @pl.when(has_below)
+        def _():
+            pl.semaphore_signal(barrier, inc=1, device_id={"lat": band - 1}, device_id_type=MESH)
+
+        @pl.when(has_above)
+        def _():
+            pl.semaphore_signal(barrier, inc=1, device_id={"lat": band + 1}, device_id_type=MESH)
+
+        peers = jnp.where(has_below, 1, 0) + jnp.where(has_above, 1, 0)
+        pl.semaphore_wait(barrier, groups - 1 + peers)
+        for index in range(chunk_count):
+
+            @pl.when(has_below)
+            def _():
+                to_lower(index).start()
+
+            @pl.when(has_above)
+            def _():
+                to_upper(index).start()
+
+    @pl.when(has_below)
+    def _():
+        to_upper(chunk).wait_recv()
+
+    @pl.when(has_above)
+    def _():
+        to_lower(chunk).wait_recv()
+
     gain = gain_ref[...]
     half_below = jnp.where(has_below, 0.5, 0.0).astype(F32)
     half_above = jnp.where(has_above, 0.5, 0.0).astype(F32)
 
-    def normed(ref, member):
-        values = ref[member].astype(F32).reshape(rows // 8, 8, width)
+    def normed(values):
+        values = values.astype(F32).reshape(rows // 8, 8, width)
         square = jnp.sum(values * values, axis=0)
         square = square + pltpu.roll(square, 2, 0)
         square = square + pltpu.roll(square, 4, 0)
@@ -186,24 +161,31 @@
         return ((half * value) * (1.0 + jnp.tanh(inner))).astype(BF16)
 
     pair = 2
+    slots = stack.shape[0]
     half_rows = entry_ref.shape[0] // 2
     depth = entry_ref.shape[1] // 2
-    for first in range(0, members, pair):
+
+    def convolve(first, slot):
         for which in range(pair):
             lanes = slice(which * width, (which + 1) * width)
-            for block, (ref, valid) in enumerate(
-                ((below_ref, has_below), (own_ref, None), (above_ref, has_above))
+            member = first + which
+            for block, (read, valid) in enumerate(
+                (
+                    (lambda: below_ref[chunk * members + member], has_below),
+                    (lambda: own_ref[member], None),
+                    (lambda: above_ref[chunk * members + member], has_above),
+                )
             ):
-                value = normed(ref, first + which)
+                value = normed(read())
                 if valid is not None:
                     value = jnp.where(valid, value, 0.0)
                 for tap in range(3):
                     moved = value if tap == 1 else pltpu.roll(value, (1 - tap) % width, 1)
                     start = block * depth + tap * rows
-                    stack[start : start + rows, lanes] = moved.astype(BF16)
+                    stack[slot, start : start + rows, lanes] = moved.astype(BF16)
         entry = entry_ref[...]
-        low = jnp.dot(entry, stack[: 2 * depth, :], preferred_element_type=F32)
-        high = jnp.dot(entry, stack[depth:, :], preferred_element_type=F32)
+        low = jnp.dot(entry, stack[slot, : 2 * depth, :], preferred_element_type=F32)
+        high = jnp.dot(entry, stack[slot, depth:, :], preferred_element_type=F32)
         hidden = jnp.concatenate(
             [
                 gelu(low[:half_rows], half_below),
@@ -220,15 +202,21 @@
             for tap in range(3):
                 part = products[tap * rows : (tap + 1) * rows, lanes]
                 total = total + (part if tap == 1 else pltpu.roll(part, (1 - tap) % width, 1))
-            field[(first + which) * rows : (first + which + 1) * rows, :] = total
+            field[pl.ds(pl.multiple_of((first + which) * rows, rows), rows), :] = total
+
+    @pl.loop(0, members // (pair * slots))
+    def _(turn):
+        for slot in range(slots):
+            convolve((turn * slots + slot) * pair, slot)
 
     columns = width // groups
     lane_group = lax.broadcasted_iota(jnp.int32, (members, width), 1) // columns
-    pieces = rows // (2 * groups)
-    for piece in range(pieces):
+
+    @pl.loop(0, rows // (2 * groups))
+    def _(piece):
         for line in range(2):
             tiles = [
-                field[pl.ds(piece * groups * 2 + inner * 2 + line, members, stride=rows), :]
+                field[pl.ds(piece * (groups * 2) + (inner * 2 + line), members, stride=rows), :]
                 for inner in range(groups)
             ]
             step = 1
@@ -245,28 +233,62 @@
                 tiles = turned
                 step *= 2
             for group in range(groups):
-                parts_ref[group, piece * 2 + line] = tiles[group].astype(BF16)
-
-
-def forecast(own, below, above, gain, entry, closing, groups):
+                parts_ref[chunk, group, piece * 2 + line] = tiles[group].astype(BF16)
+
+    for step in range(1, groups):
+        to_group(chunk, step).start()
+    to_self(chunk).start()
+
+    @pl.when(chunk == chunks - 1)
+    def _():
+        for index in range(chunk_count):
+
+            @pl.when(has_below)
+            def _():
+                to_lower(index).wait_send()
+
+            @pl.when(has_above)
+            def _():
+                to_upper(index).wait_send()
+
+            for step in range(1, groups):
+                to_group(index, step).wait()
+            to_self(index).wait()
+
+
+def forecast(own, gain, entry, closing, groups):
     members, rows, width = own.shape
     chunk = min(16, members)
+    chunks = members // chunk
     pieces = rows // groups
-    block = pl.BlockSpec((chunk, rows, width), lambda i: (i, 0, 0))
     whole = lambda a: pl.BlockSpec(a.shape, lambda i: (0,) * a.ndim)
+    anywhere = pl.BlockSpec(memory_space=pl.ANY)
     return pl.pallas_call(
-        functools.partial(forecast_kernel, groups),
+        forecast_kernel,
         out_shape=jax.ShapeDtypeStruct((groups, pieces, members, width), BF16),
-        grid=(members // chunk,),
-        in_specs=[block, block, block, whole(gain), whole(entry), whole(closing)],
-        out_specs=pl.BlockSpec((groups, pieces, chunk, width), lambda i: (0, 0, i, 0)),
+        grid=(chunks,),
+        in_specs=[
+            pl.BlockSpec((chunk, rows, width), lambda i: (i, 0, 0)),
+            whole(gain), whole(entry), whole(closing), anywhere,
+        ],
+        out_specs=anywhere,
         scratch_shapes=[
-            pltpu.VMEM((9 * rows, 2 * width), BF16),
+            pltpu.VMEM((members, rows, width), BF16),
+            pltpu.VMEM((members, rows, width), BF16),
+            pltpu.VMEM((chunks, groups, pieces, chunk, width), BF16),
+            pltpu.VMEM((2, 9 * rows, 2 * width), BF16),
             pltpu.VMEM((chunk * rows, width), F32),
+            pltpu.SemaphoreType.DMA((2, chunks)),
+            pltpu.SemaphoreType.DMA((2, chunks)),
+            pltpu.SemaphoreType.DMA((chunks, groups)),
+            pltpu.SemaphoreType.DMA((chunks, groups)),
+            pltpu.SemaphoreType.DMA((chunks,)),
         ],
-        compiler_params=pltpu.CompilerParams(vmem_limit_bytes=VMEM_LIMIT),
+        compiler_params=pltpu.CompilerParams(
+            vmem_limit_bytes=VMEM_LIMIT, collective_id=0, has_side_effects=True
+        ),
         name="forecast",
-    )(own, below, above, gain, entry, closing)
+    )(own, gain, entry, closing, own)
 
 
 def observe_kernel(got_ref, operator_ref, value_ref, precision_ref, out_ref):
@@ -434,9 +456,7 @@
     value = jnp.broadcast_to(observed_value[0, 0][:, None], (observations, LANES))
     precision = jnp.broadcast_to(observed_precision[0, 0][:, None], (observations, LANES))
 
-    below, above = halo_exchange(own)
-    parts = forecast(own, below, above, gain, entry, closing, groups)
-    got = exchange(parts)
+    got = forecast(own, gain, entry, closing, groups)
     mine = observe(got, operator, value, precision)
     gathered = gather(mine, groups)
     gathered = gathered.reshape(groups * observations, mine.shape[1])

time: 130 us -> 107 us (0.82); the launches traced: 127 us -> 107 us
  Pallas kernels: 118 us -> 94.1 us
  local copies, waits for them, and re-layouts: 8.36 us -> 10.9 us
    pallas_call x3 -> x1, Pallas kernels: 84.4 us -> 66 us  [forecast(): pl.pallas_call(forecast_kernel, out_shape=jax.ShapeDtypeStruct((groups, p...]
    pallas_call x1, Pallas kernels: 17 us -> 11.7 us  [gather(): pl.pallas_call(gather_kernel, out_shape=jax.ShapeDtypeStruct((count,) + m...]
where the time goes in v1:
time: 107 us
  Pallas kernels  94.1 us (88%)
  local copies, waits for them, and re-layouts  10.9 us (10%)
  other arithmetic  1.53 us (1%)
    pallas_call x1, Pallas kernels, forecast(): pl.pallas_call(forecast_kernel, out_shape=jax.ShapeDtypeStruct((groups, p...  66 us
    pallas_call x1, Pallas kernels, analyse(): pl.pallas_call(analyse_kernel, out_shape=jax.ShapeDtypeStruct((columns, 2...  13.3 us
    pallas_call x1, Pallas kernels, gather(): pl.pallas_call(gather_kernel, out_shape=jax.ShapeDtypeStruct((count,) + m...  11.7 us
    pallas_call x1, Pallas kernels, observe(): pl.pallas_call(observe_kernel, out_shape=jax.ShapeDtypeStruct((observatio...  3.08 us

profile of v1, /device:TPU:1, one launch (start us, length us, event | category | flops | bytes accessed | tf_op | source)
XLA Modules:
  0.0 106.6 jit_solution(3016509114194543516)
XLA Ops:
  0.0 1.3 %broadcast_in_dim.31.value_ref = f32[16,128]{1,0:T(8,128)} broadcast(f32[16]{0:T(128)} %bitcast.41), dimensions={0} | broadcast | bytes 8256 | tf_op jit(solution)/shard_map/broadcast_in_dim | solution.py:456
  1.3 1.3 %broadcast_in_dim.33.precision_ref = f32[16,128]{1,0:T(8,128)} broadcast(f32[16]{0:T(128)} %bitcast.42), dimensions={0} | broadcast | bytes 8256 | tf_op jit(solution)/shard_map/broadcast_in_dim | solution.py:457
  2.6 0.7 compare_convert_fusion
  3.4 0.7 broadcast_in_dim.27
  4.1 0.1 broadcast_in_dim.28
  4.2 0.8 copy.16
  5.0 0.1 copy.17
  5.1 0.7 broadcast_in_dim.29.gain_ref
  5.8 1.2 %copy.13 = bf16[3,3,64,256]{3,0,2,1:T(4,128)(2,1)S(1)} copy(bf16[3,3,64,256]{3,2,1,0:T(8,128)(2,1)} %bitcast.38) | data formatting | bytes 589824 | tf_op jit(solution)/shard_map/reshape | solution.py:444
  7.0 0.0 copy-start
  7.0 0.4 pad_bitcast_fusion.1
  7.4 0.5 pad_maximum_fusion
  7.9 1.1 %copy.19 = bf16[48,8,4,256]{3,1,2,0:T(8,128)(2,1)} copy(bf16[48,8,4,256]{3,2,1,0:T(4,128)(2,1)S(1)} %bitcast.31) | data formatting | bytes 1572864
  9.0 0.0 copy-done
  9.0 0.1 fusion
  9.1 0.1 maximum_bitcast_fusion
  9.2 0.8 copy.12
  10.0 0.2 copy.18
  10.1 1.2 %copy.15.entry_ref = bf16[512,768]{1,0:T(8,128)(2,1)} copy(bf16[512,768]{0,1:T(8,128)(2,1)S(1)} %bitcast.33) | data formatting | bytes 1572864 | tf_op jit(solution)/shard_map/reshape | solution.py:443
  11.3 66.0 %forecast.1.got_ref = bf16[8,16,64,128]{3,2,1,0:T(8,128)(2,1)} custom-call(bf16[64,128,128]{2,1,0:T(8,128)(2,1)} %bitcast.29, f32[128,128]{1,0:T(8,128)} %broadcast_in_dim.29.gain_ref, bf16[512,768]{1,0:T(8,128)(2,1)} %copy.15.entry_ref, bf16[384,1024]{1,0:T(8,128)(2,1)} %bitcast.34, bf16[64,128,128]{2,1,0:T(8,128)(2,1)} %bitcast.30), custom_call_target="tpu_custom_call" | custom-call | tf_op jit(solution)/shard_map/forecast/pallas_call | solution.py:266
  77.3 0.2 broadcast_multiply_fusion
  77.5 1.0 mul.20.operator_ref
  78.5 3.1 %observe.1.mine_ref = f32[16,640]{1,0:T(8,128)} custom-call(bf16[8,16,64,128]{3,2,1,0:T(8,128)(2,1)} %forecast.1.got_ref, f32[16,16,128]{2,1,0:T(8,128)} %mul.20.operator_ref, f32[16,128]{1,0:T(8,128)} %broadcast_in_dim.31.value_ref, f32[16,128]{1,0:T(8,128)} %broadcast_in_dim.33.precision_ref), custom_call_target="tpu_custom_call" | custom-call | tf_op jit(solution)/shard_map/observe/pallas_call | solution.py:320
  81.6 11.7 %gather.1 = f32[8,16,640]{2,1,0:T(8,128)} custom-call(f32[16,640]{1,0:T(8,128)} %observe.1.mine_ref), custom_call_target="tpu_custom_call" | custom-call | tf_op jit(solution)/shard_map/gather/pallas_call | solution.py:52
  93.3 13.3 %analyse.1 = f32[16,2,64,512]{3,2,1,0:T(8,128)} custom-call(bf16[8,16,64,128]{3,2,1,0:T(8,128)(2,1)} %forecast.1.got_ref, f32[128,640]{1,0:T(8,128)} %bitcast.37), custom_call_target="tpu_custom_call" | custom-call | tf_op jit(solution)/shard_map/analyse/pallas_call | solution.py:404
  (1 shorter events, 0.0 us)
Async XLA Ops:
  7.0 2.0 %copy-start = (bf16[9,256,64]{1,2,0:T(8,128)(2,1)S(1)}, bf16[9,256,64]{1,2,0:T(8,128)(2,1)}, u32[]{:S(2)}) copy-start(bf16[9,256,64]{1,2,0:T(8,128)(2,1)} %param.10) | copy-start | bytes 884740

commit v2 on v1

--- a/solution.py
+++ b/solution.py
@@ -15,53 +15,6 @@
 F32 = jnp.float32
 BF16 = jnp.bfloat16
 highest = lax.Precision.HIGHEST
-
-
-def greet_all(axis):
-    count = lax.axis_size(axis)
-    me = lax.axis_index(axis)
-    barrier = pltpu.get_barrier_semaphore()
-    for step in range(1, count):
-        pl.semaphore_signal(
-            barrier, inc=1, device_id={axis: lax.rem(me + step, count)}, device_id_type=MESH
-        )
-    pl.semaphore_wait(barrier, count - 1)
-
-
-def gather_kernel(mine_ref, all_ref, send_sem, recv_sem, own_sem):
-    count = lax.axis_size("mem")
-    me = lax.axis_index("mem")
-    greet_all("mem")
-    copies = []
-    for step in range(1, count):
-        other = lax.rem(me + step, count)
-        copy = pltpu.make_async_remote_copy(
-            mine_ref, all_ref.at[me], send_sem.at[step], recv_sem.at[step],
-            device_id={"mem": other}, device_id_type=MESH,
-        )
-        copy.start()
-        copies.append(copy)
-    keep = pltpu.make_async_copy(mine_ref, all_ref.at[me], own_sem)
-    keep.start()
-    keep.wait()
-    for copy in copies:
-        copy.wait()
-
-
-def gather(mine, count):
-    return pl.pallas_call(
-        gather_kernel,
-        out_shape=jax.ShapeDtypeStruct((count,) + mine.shape, mine.dtype),
-        in_specs=[pl.BlockSpec(memory_space=pltpu.VMEM)],
-        out_specs=pl.BlockSpec(memory_space=pltpu.VMEM),
-        scratch_shapes=[
-            pltpu.SemaphoreType.DMA((count,)),
-            pltpu.SemaphoreType.DMA((count,)),
-            pltpu.SemaphoreType.DMA,
-        ],
-        compiler_params=pltpu.CompilerParams(collective_id=2, has_side_effects=True),
-        name="gather",
-    )(mine)
 
 
 def forecast_kernel(
@@ -161,7 +114,7 @@
         return ((half * value) * (1.0 + jnp.tanh(inner))).astype(BF16)
 
     pair = 2
-    slots = stack.shape[0]
+    slots = min(stack.shape[0], members // pair)
     half_rows = entry_ref.shape[0] // 2
     depth = entry_ref.shape[1] // 2
 
@@ -276,7 +229,7 @@
             pltpu.VMEM((members, rows, width), BF16),
             pltpu.VMEM((members, rows, width), BF16),
             pltpu.VMEM((chunks, groups, pieces, chunk, width), BF16),
-            pltpu.VMEM((2, 9 * rows, 2 * width), BF16),
+            pltpu.VMEM((4, 9 * rows, 2 * width), BF16),
             pltpu.VMEM((chunk * rows, width), F32),
             pltpu.SemaphoreType.DMA((2, chunks)),
             pltpu.SemaphoreType.DMA((2, chunks)),
@@ -291,7 +244,16 @@
     )(own, gain, entry, closing, own)
 
 
-def observe_kernel(got_ref, operator_ref, value_ref, precision_ref, out_ref):
+def observe_kernel(
+    got_ref, operator_ref, value_ref, precision_ref, all_ref, out_ref, send_sem, recv_sem, own_sem
+):
+    count = lax.axis_size("mem")
+    me = lax.axis_index("mem")
+    barrier = pltpu.get_barrier_semaphore()
+    for step in range(1, count):
+        pl.semaphore_signal(
+            barrier, inc=1, device_id={"mem": lax.rem(me + step, count)}, device_id_type=MESH
+        )
     sources, pieces, part, width = got_ref.shape
     observations = operator_ref.shape[1]
     total = None
@@ -312,15 +274,37 @@
     root = jnp.sqrt(precision_ref[...])
     out_ref[:, : sources * part] = (seen - mean) * root[:, :1]
     out_ref[:, sources * part :] = (value_ref[...] - mean) * root
+    pl.semaphore_wait(barrier, count - 1)
+    copies = []
+    for step in range(1, count):
+        copy = pltpu.make_async_remote_copy(
+            out_ref, all_ref.at[me], send_sem.at[step], recv_sem.at[step],
+            device_id={"mem": lax.rem(me + step, count)}, device_id_type=MESH,
+        )
+        copy.start()
+        copies.append(copy)
+    keep = pltpu.make_async_copy(out_ref, all_ref.at[me], own_sem)
+    keep.start()
+    keep.wait()
+    for copy in copies:
+        copy.wait()
 
 
 def observe(got, operator, value, precision):
     sources, _, part, width = got.shape
-    observations = operator.shape[1]
+    mine = (operator.shape[1], sources * part + LANES)
     return pl.pallas_call(
         observe_kernel,
-        out_shape=jax.ShapeDtypeStruct((observations, sources * part + LANES), F32),
-        compiler_params=pltpu.CompilerParams(vmem_limit_bytes=VMEM_LIMIT),
+        out_shape=jax.ShapeDtypeStruct((sources,) + mine, F32),
+        scratch_shapes=[
+            pltpu.VMEM(mine, F32),
+            pltpu.SemaphoreType.DMA((sources,)),
+            pltpu.SemaphoreType.DMA((sources,)),
+            pltpu.SemaphoreType.DMA,
+        ],
+        compiler_params=pltpu.CompilerParams(
+            vmem_limit_bytes=VMEM_LIMIT, collective_id=2, has_side_effects=True
+        ),
         name="observe",
     )(got, operator, value, precision)
 
@@ -457,9 +441,8 @@
     precision = jnp.broadcast_to(observed_precision[0, 0][:, None], (observations, LANES))
 
     got = forecast(own, gain, entry, closing, groups)
-    mine = observe(got, operator, value, precision)
-    gathered = gather(mine, groups)
-    gathered = gathered.reshape(groups * observations, mine.shape[1])
+    gathered = observe(got, operator, value, precision)
+    gathered = gathered.reshape(groups * observations, gathered.shape[2])
     return analyse(got, gathered, columns, variables)
 
 

time: 107 us -> 105 us (0.981)
  Pallas kernels: 94.1 us -> 91.4 us
    pallas_call x2 -> x1, Pallas kernels: 14.8 us -> 13.2 us  [observe(): pl.pallas_call(observe_kernel, out_shape=jax.ShapeDtypeStruct((sources,)...]
    pallas_call x1, Pallas kernels: 66 us -> 64.9 us  [forecast(): pl.pallas_call(forecast_kernel, out_shape=jax.ShapeDtypeStruct((groups, p...]
where the time goes in v2:
time: 105 us; the launch traced here: 104 us
  Pallas kernels  91.4 us (87%)
  local copies, waits for them, and re-layouts  10.9 us (10%)
  other arithmetic  1.53 us (1%)
    pallas_call x1, Pallas kernels, forecast(): pl.pallas_call(forecast_kernel, out_shape=jax.ShapeDtypeStruct((groups, p...  64.9 us
    pallas_call x1, Pallas kernels, analyse(): pl.pallas_call(analyse_kernel, out_shape=jax.ShapeDtypeStruct((columns, 2...  13.3 us
    pallas_call x1, Pallas kernels, observe(): pl.pallas_call(observe_kernel, out_shape=jax.ShapeDtypeStruct((sources,)...  13.2 us

profile of v2, /device:TPU:1, one launch (start us, length us, event | category | flops | bytes accessed | tf_op | source)
XLA Modules:
  0.0 103.9 jit_solution(17422067619217178125)
XLA Ops:
  0.0 1.3 %broadcast_in_dim.31.value_ref = f32[16,128]{1,0:T(8,128)} broadcast(f32[16]{0:T(128)} %bitcast.41), dimensions={0} | broadcast | bytes 8256 | tf_op jit(solution)/shard_map/broadcast_in_dim | solution.py:440
  1.3 1.3 %broadcast_in_dim.33.precision_ref = f32[16,128]{1,0:T(8,128)} broadcast(f32[16]{0:T(128)} %bitcast.42), dimensions={0} | broadcast | bytes 8256 | tf_op jit(solution)/shard_map/broadcast_in_dim | solution.py:441
  2.6 0.7 compare_convert_fusion
  3.4 0.7 broadcast_in_dim.27
  4.1 0.1 broadcast_in_dim.28
  4.2 0.8 copy.16
  5.0 0.1 copy.17
  5.1 0.7 broadcast_in_dim.29.gain_ref
  5.8 1.2 %copy.13 = bf16[3,3,64,256]{3,0,2,1:T(4,128)(2,1)S(1)} copy(bf16[3,3,64,256]{3,2,1,0:T(8,128)(2,1)} %bitcast.38) | data formatting | bytes 589824 | tf_op jit(solution)/shard_map/reshape | solution.py:428
  7.0 0.0 copy-start
  7.0 0.4 pad_bitcast_fusion.1
  7.4 0.5 pad_maximum_fusion
  7.9 1.1 %copy.19 = bf16[48,8,4,256]{3,1,2,0:T(8,128)(2,1)} copy(bf16[48,8,4,256]{3,2,1,0:T(4,128)(2,1)S(1)} %bitcast.31) | data formatting | bytes 1572864
  9.0 0.0 copy-done
  9.0 0.1 fusion
  9.1 0.1 maximum_bitcast_fusion
  9.2 0.8 copy.12
  10.0 0.2 copy.18
  10.1 1.2 %copy.15.entry_ref = bf16[512,768]{1,0:T(8,128)(2,1)} copy(bf16[512,768]{0,1:T(8,128)(2,1)S(1)} %bitcast.33) | data formatting | bytes 1572864 | tf_op jit(solution)/shard_map/reshape | solution.py:427
  11.3 64.9 %forecast.1.got_ref = bf16[8,16,64,128]{3,2,1,0:T(8,128)(2,1)} custom-call(bf16[64,128,128]{2,1,0:T(8,128)(2,1)} %bitcast.29, f32[128,128]{1,0:T(8,128)} %broadcast_in_dim.29.gain_ref, bf16[512,768]{1,0:T(8,128)(2,1)} %copy.15.entry_ref, bf16[384,1024]{1,0:T(8,128)(2,1)} %bitcast.34, bf16[64,128,128]{2,1,0:T(8,128)(2,1)} %bitcast.30), custom_call_target="tpu_custom_call" | custom-call | tf_op jit(solution)/shard_map/forecast/pallas_call | solution.py:219
  76.2 0.2 broadcast_multiply_fusion
  76.4 1.0 mul.20.operator_ref
  77.4 13.2 %observe.1 = f32[8,16,640]{2,1,0:T(8,128)} custom-call(bf16[8,16,64,128]{3,2,1,0:T(8,128)(2,1)} %forecast.1.got_ref, f32[16,16,128]{2,1,0:T(8,128)} %mul.20.operator_ref, f32[16,128]{1,0:T(8,128)} %broadcast_in_dim.31.value_ref, f32[16,128]{1,0:T(8,128)} %broadcast_in_dim.33.precision_ref), custom_call_target="tpu_custom_call" | custom-call | tf_op jit(solution)/shard_map/observe/pallas_call | solution.py:296
  90.6 13.3 %analyse.1 = f32[16,2,64,512]{3,2,1,0:T(8,128)} custom-call(bf16[8,16,64,128]{3,2,1,0:T(8,128)(2,1)} %forecast.1.got_ref, f32[128,640]{1,0:T(8,128)} %bitcast.37), custom_call_target="tpu_custom_call" | custom-call | tf_op jit(solution)/shard_map/analyse/pallas_call | solution.py:388
  (1 shorter events, 0.0 us)
Async XLA Ops:
  7.0 2.0 %copy-start = (bf16[9,256,64]{1,2,0:T(8,128)(2,1)S(1)}, bf16[9,256,64]{1,2,0:T(8,128)(2,1)}, u32[]{:S(2)}) copy-start(bf16[9,256,64]{1,2,0:T(8,128)(2,1)} %param.10) | copy-start | bytes 884740
